TPU v7x, 32 devices: a whole 2x2x4 slice. The times are simulated.
32 devices in a mesh: ens: 2 (over y), lon: 4 (over z), dom: 4 (over x, core).
Axes of the slice: x: 2, y: 2, z: 4, core: 2. Of those that a mesh axis runs over, the one named last changes fastest.
Arguments:
- particles: bfloat16 [16, 69, 96, 256], P(('ens', 'dom'), None, 'lon'), parts along dimension 0, may hold values from -6 to 6
- observed: bfloat16 [138, 96, 256], P('ens', 'lon'), parts along dimension 0, may hold values from -6 to 6
- precision: float32 [192, 256], P(('ens', 'lon')), parts along dimension 0, may hold values from 0.25 to 12, as said below
- stations: int32 [192, 256], P(('ens', 'lon')), parts along dimension 0, may hold values 0 or 1
- ancestors: int32 [16], P(('ens', 'dom')), parts along dimension 0, may hold values from 0 to 7
- tempering: float32 [2], P('ens'), parts along dimension 0, may hold values from 1 to 4
- w_in: bfloat16 [3, 3, 64, 69], replicated, may hold values from -0.25 to 0.25
- w_mid: bfloat16 [3, 3, 64, 64], replicated, may hold values from -0.25 to 0.25
- w_out: bfloat16 [3, 3, 69, 64], replicated, may hold values from -0.25 to 0.25
Outputs:
- new_particles: bfloat16 [16, 69, 96, 256], P(('ens', 'dom'), None, 'lon'), parts along dimension 0
- weights: float32 [16], P(('ens', 'dom')), parts along dimension 0
There are 2 independent parts, one for each index of `ens`. A program takes and returns all parts, laid end to end along the dimension named above; an argument that names none is the same for every part. Nothing has to cross between parts.
Inputs may be any that keep to these rules, and one draw needn't show every extreme that they name: `precision`: positive everywhere; no other structure is promised. Slot s continues particle ancestors[s]; a particle may be continued by several slots or by none.
All inputs are finite; a program needn't handle non-finite values. No bound on the sum of `stations` on one device may be relied on, other than what follows from the above.
Results may differ from a plain program's by a relative error of at most 0.0021.
Values may be sent and summed in bfloat16 or wider, within the bound.
A program may use at most 128 MiB of HBM per device.

v0:
```python
import jax
import jax.numpy as jnp
from jax import lax
from jax.sharding import PartitionSpec as P


def extended_2(block, sides, width):
    for axis, dim in sides:
        count = lax.axis_size(axis)
        forward = [(i, i + 1) for i in range(count - 1)]
        forward.append((count - 1, 0))
        backward = [(target, source) for source, target in forward]
        low = lax.ppermute(
            lax.slice_in_dim(block, block.shape[dim] - width, None, axis=dim), axis, forward
        )
        high = lax.ppermute(lax.slice_in_dim(block, 0, width, axis=dim), axis, backward)
        block = jnp.concatenate([low, block, high], axis=dim)
    return block


def conv_local(extended, weight):
    out_width = extended.shape[2] - 2
    lat_rows = extended.shape[3]
    padded = jnp.pad(extended, ((0, 0), (0, 0), (0, 0), (1, 1)))
    summed = jnp.zeros((extended.shape[0], weight.shape[2], out_width, lat_rows), jnp.float32)
    for row_tap in range(3):
        for col_tap in range(3):
            window = padded[:, :, row_tap : row_tap + out_width, col_tap : col_tap + lat_rows]
            summed = summed + jnp.einsum(
                "oc,pcxy->poxy",
                weight[row_tap, col_tap],
                window,
                preferred_element_type=jnp.float32,
            )
    return summed


def denoise_local(states, observed, obs_weight, w_in, w_mid, w_out):
    extended = extended_2(states, (("lon", 2),), 1)
    first_act = jax.nn.silu(conv_local(extended, w_in)).astype(jnp.bfloat16)
    first_ext = extended_2(first_act, (("lon", 2),), 1)
    second_act = jax.nn.silu(conv_local(first_ext, w_mid)).astype(jnp.bfloat16)
    second_ext = extended_2(second_act, (("lon", 2),), 1)
    noise_pred = conv_local(second_ext, w_out)
    current = states.astype(jnp.float32)
    updated = (
        current
        - 0.5 * noise_pred
        + 0.25 * obs_weight[None, None] * (observed.astype(jnp.float32)[None] - current)
    )
    return updated.astype(jnp.bfloat16)


def continue_slots(slabs, slot_ancestors):
    slab_piece = lax.all_gather(slabs, "dom", axis=0, tiled=True)
    piece_rows = slab_piece.shape[0]
    inside = (slot_ancestors >= 0) & (slot_ancestors < piece_rows)
    chosen = jnp.take(slab_piece, jnp.clip(slot_ancestors, 0, piece_rows - 1), axis=0)
    return jnp.where(inside[:, None, None, None], chosen, jnp.zeros_like(slabs))


def on_device(particles, observed, precision, stations, ancestors, tempering, w_in, w_mid, w_out):
    obs_weight = stations.astype(jnp.float32) * precision
    misfit_cell = particles.astype(jnp.float32) - observed.astype(jnp.float32)[None]
    local_sums = jnp.sum(obs_weight[None, None] * misfit_cell * misfit_cell, axis=(1, 2, 3))
    band_sums = lax.psum(local_sums, "lon")
    every_sum = lax.all_gather(band_sums, "dom", axis=0, tiled=True)
    center = jnp.mean(every_sum)
    deviation = every_sum - center
    spread = jnp.sqrt(jnp.mean(deviation * deviation) + 1.0)
    log_weights = -0.5 * tempering[0] * deviation / spread
    expo = jnp.exp(log_weights)
    weights_all = expo / jnp.sum(expo)
    slot_count = ancestors.shape[0]
    own_weights = lax.dynamic_slice_in_dim(
        weights_all, lax.axis_index("dom") * slot_count, slot_count
    )
    continued = continue_slots(particles, ancestors)
    new_particles = denoise_local(continued, observed, obs_weight, w_in, w_mid, w_out)
    return (new_particles, own_weights)


def solution(mesh):
    return jax.shard_map(
        on_device,
        mesh=mesh,
        in_specs=(
            P(("ens", "dom"), None, "lon", None),
            P("ens", "lon", None),
            P(("ens", "lon"), None),
            P(("ens", "lon"), None),
            P(("ens", "dom")),
            P("ens"),
            P(),
            P(),
            P(),
        ),
        out_specs=(P(("ens", "dom"), None, "lon", None), P(("ens", "dom"))),
        check_vma=False,
    )
```

profile of v0, /device:TPU:0, one launch (start us, length us, event | category | flops | bytes accessed | tf_op | source)
XLA Modules:
  0.0 159.0 jit_solution(17750243368687318687)
XLA Ops:
  10.2 13.4 %psum.7 = f32[2]{0:T(128)S(1)} all-reduce(f32[2]{0:T(128)S(1)} %fusion.5), channel_id=1, replica_groups=mesh['ens'=2,'lon'=4,'dom'=4] {'lon'}, use_global_device_ids=true, to_apply=%region_1.0 | all-reduce | flops 2 | bytes 16 | tf_op jit(solution)/shard_map/psum | solution.py:66
  25.1 6.1 %all-reduce.3 = f32[8]{0:T(128)S(1)} all-reduce(f32[8]{0:T(128)S(1)} %dynamic-update-slice), channel_id=1, replica_groups=mesh['ens'=2,'lon'=4,'dom'=4] {'dom'}, use_global_device_ids=true, to_apply=%add.3 | all-reduce | flops 8 | bytes 64
  36.4 25.2 %all-gather.2.cloned.1.call-done = bf16[8,69,24,256]{3,2,1,0:T(8,128)(2,1)} async-done(((bf16[2,69,24,256]{3,2,1,0:T(8,128)(2,1)}), bf16[8,69,24,256]{3,2,1,0:T(8,128)(2,1)}) %all-gather.2.cloned.1.call-update) | async-done | bytes 6782992 | tf_op jit(solution)/shard_map/all_gather | solution.py:55
  61.6 3.6 %gather_fusion = bf16[2,69,24,256]{3,2,1,0:T(8,128)(2,1)S(1)} fusion(bf16[8,69,24,256]{3,2,1,0:T(8,128)(2,1)} %all-gather.2.cloned.1.call-done, s32[1024]{0:T(1024)S(1)} %pad_clamp_fusion), kind=kCustom, calls=%fused_computation | custom fusion | bytes 3391496 | tf_op jit(solution)/shard_map/jit(_take)/gather | solution.py:58
  67.2 2.3 %collective-permute-start.1 = (bf16[2,69,1,256]{3,1,2,0:T(8,128)(2,1)S(1)}, bf16[2,69,1,256]{3,1,2,0:T(8,128)(2,1)S(1)}, u32[]{:S(2)}, u32[]{:S(2)}) collective-permute-start(bf16[2,69,1,256]{3,1,2,0:T(8,128)(2,1)S(1)} %get-tuple-element.15), channel_id=1, source_target_pairs={{4,0},{8,4},{12,8},{0,12},{5,1},{9,5},{13,9},{1,13},{6,2},{10,6},{... | collective-permute-start | bytes 211976 | tf_op jit(solution)/shard_map/ppermute | solution.py:16
  69.6 2.6 %fusion.111 = f32[2,24,256,64]{2,3,1,0:T(8,128)} fusion(bf16[3,3,64,69]{3,2,1,0:T(8,128)(2,1)S(1)} %copy-done.3, bf16[2,69,24,256]{3,2,1,0:T(8,128)(2,1)S(1)} %gather_fusion, pred[2]{0:T(512)(128)(4,1)S(1)} %get-tuple-element.12, pred[2]{0:T(512)(128)(4,1)S(1)} %get-tuple-element.20), kind=kOutput, calls=%fused_computation.123 | convolution fusion | flops 110223360 | bytes 4858880 | tf_op jit(solution)/shard_map/oc,pcxy->poxy/dot_general | solution.py:29
  77.8 2.2 %fusion.42 = f32[2,24,256,64]{2,3,1,0:T(8,128)} fusion(bf16[2,69,26,258]{3,1,2,0:T(8,128)(2,1)S(1)} %fusion.18, bf16[3,3,64,69]{3,2,1,0:T(8,128)(2,1)S(1)} %copy-done.3), kind=kOutput, calls=%fused_computation.56 | convolution fusion | flops 108527616 | bytes 4931584 | tf_op jit(solution)/shard_map/oc,pcxy->poxy/dot_general | solution.py:29
  80.0 2.2 %fusion.24 = f32[2,24,256,64]{2,3,1,0:T(8,128)} fusion(bf16[2,69,24,256]{3,1,2,0:T(8,128)(2,1)S(1)} %fusion.44, bf16[2,69,1,256]{3,1,2,0:T(8,128)(2,1)S(1)} %collective-permute-done, bf16[3,3,64,69]{3,2,1,0:T(8,128)(2,1)S(1)} %copy-done.3), kind=kOutput, calls=%fused_computation.38 | convolution fusion | flops 112060416 | bytes 5005312 | tf_op jit(solution)/shard_map/oc,pcxy->poxy/dot_general | solution.py:29
  82.2 2.2 %fusion.28 = f32[2,24,256,64]{2,3,1,0:T(8,128)} fusion(bf16[2,69,1,256]{3,1,2,0:T(8,128)(2,1)S(1)} %collective-permute-done.1, bf16[2,69,24,256]{3,1,2,0:T(8,128)(2,1)S(1)} %fusion.44, bf16[3,3,64,69]{3,2,1,0:T(8,128)(2,1)S(1)} %copy-done.3), kind=kOutput, calls=%fused_computation.42 | convolution fusion | flops 112060416 | bytes 5005312 | tf_op jit(solution)/shard_map/oc,pcxy->poxy/dot_general | solution.py:29
  84.4 6.0 %fusion.15 = bf16[2,64,24,256]{3,1,2,0:T(8,128)(2,1)S(1)} fusion(f32[2,24,256,64]{2,3,1,0:T(8,128)} %fusion.28, f32[2,24,256,64]{2,3,1,0:T(8,128)S(1)} %fusion.34, f32[2,24,256,64]{2,3,1,0:T(8,128)S(1)} %fusion.36, f32[2,24,256,64]{2,3,1,0:T(8,128)} %fusion.111, f32[2,24,256,64]{2,3,1,0:T(8,128)S(1)} %fusion.38, f32[2,24,256,64]{2,3,1,0:T(8,128)S(1)} %fusion.40, ...), kind=kOutput, calls=%fused_computation.27 | convolution fusion | flops 118751232 | bytes 28524544 | tf_op jit(solution)/shard_map/oc,pcxy->poxy/dot_general | solution.py:29
  91.6 2.7 %collective-permute-start.3 = (bf16[2,64,1,256]{3,1,2,0:T(8,128)(2,1)S(1)}, bf16[2,64,1,256]{3,1,2,0:T(8,128)(2,1)S(1)}, u32[]{:S(2)}, u32[]{:S(2)}) collective-permute-start(bf16[2,64,1,256]{3,1,2,0:T(8,128)(2,1)S(1)} %get-tuple-element.19), channel_id=1, source_target_pairs={{4,0},{8,4},{12,8},{0,12},{5,1},{9,5},{13,9},{1,13},{6,2},{10,6},{... | collective-permute-start | bytes 196616 | tf_op jit(solution)/shard_map/ppermute | solution.py:16
  100.4 2.3 %fusion.81 = f32[2,24,256,64]{2,3,1,0:T(8,128)} fusion(bf16[2,64,26,258]{3,1,2,0:T(8,128)(2,1)S(1)} %fusion.23, bf16[3,3,64,64]{3,2,1,0:T(8,128)(2,1)S(1)} %copy-done.1), kind=kOutput, calls=%fused_computation.91 | convolution fusion | flops 100663296 | bytes 4734976 | tf_op jit(solution)/shard_map/oc,pcxy->poxy/dot_general | solution.py:29
  102.7 2.2 %fusion.85 = f32[2,24,256,64]{2,3,1,0:T(8,128)} fusion(bf16[2,64,26,258]{3,1,2,0:T(8,128)(2,1)S(1)} %fusion.23, bf16[3,3,64,64]{3,2,1,0:T(8,128)(2,1)S(1)} %copy-done.1), kind=kOutput, calls=%fused_computation.96 | convolution fusion | flops 100663296 | bytes 4734976 | tf_op jit(solution)/shard_map/oc,pcxy->poxy/dot_general | solution.py:29
  107.1 2.2 %fusion.73 = f32[2,24,256,64]{2,3,1,0:T(8,128)} fusion(bf16[2,64,1,256]{3,1,2,0:T(8,128)(2,1)S(1)} %collective-permute-done.3, bf16[2,64,24,256]{3,1,2,0:T(8,128)(2,1)S(1)} %fusion.15, bf16[3,3,64,64]{3,2,1,0:T(8,128)(2,1)S(1)} %copy-done.1), kind=kOutput, calls=%fused_computation.83 | convolution fusion | flops 103809024 | bytes 4800512 | tf_op jit(solution)/shard_map/oc,pcxy->poxy/dot_general | solution.py:29
  109.3 5.9 %fusion.16 = bf16[2,64,24,256]{3,1,2,0:T(8,128)(2,1)S(1)} fusion(f32[2,24,256,64]{2,3,1,0:T(8,128)} %fusion.73, f32[2,24,256,64]{2,3,1,0:T(8,128)S(1)} %fusion.75, f32[2,24,256,64]{2,3,1,0:T(8,128)S(1)} %fusion.77, f32[2,24,256,64]{2,3,1,0:T(8,128)S(1)} %fusion.101, f32[2,24,256,64]{2,3,1,0:T(8,128)S(1)} %fusion.79, f32[2,24,256,64]{2,3,1,0:T(8,128)} %fusion.81, ...), kind=kOutput, calls=%fused_computation.28 | convolution fusion | flops 110886912 | bytes 28327936 | tf_op jit(solution)/shard_map/oc,pcxy->poxy/dot_general | solution.py:29
  115.9 3.3 %collective-permute-start.5 = (bf16[2,64,1,256]{3,1,2,0:T(8,128)(2,1)S(1)}, bf16[2,64,1,256]{3,1,2,0:T(8,128)(2,1)S(1)}, u32[]{:S(2)}, u32[]{:S(2)}) collective-permute-start(bf16[2,64,1,256]{3,1,2,0:T(8,128)(2,1)S(1)} %get-tuple-element.17), channel_id=1, source_target_pairs={{4,0},{8,4},{12,8},{0,12},{5,1},{9,5},{13,9},{1,13},{6,2},{10,6},{... | collective-permute-start | bytes 196616 | tf_op jit(solution)/shard_map/ppermute | solution.py:16
  123.2 2.5 %fusion.59 = f32[2,24,256,69]{2,3,1,0:T(8,128)} fusion(bf16[2,64,26,258]{3,1,2,0:T(8,128)(2,1)S(1)} %select_maximum_fusion, bf16[3,3,69,64]{2,3,1,0:T(8,128)(2,1)S(1)} %copy-done.2), kind=kOutput, calls=%fused_computation.70 | convolution fusion | flops 108527616 | bytes 4980736 | tf_op jit(solution)/shard_map/oc,pcxy->poxy/dot_general | solution.py:29
  125.7 2.6 %fusion.61 = f32[2,24,256,69]{2,3,1,0:T(8,128)} fusion(bf16[2,64,26,258]{3,1,2,0:T(8,128)(2,1)S(1)} %select_maximum_fusion, bf16[3,3,69,64]{2,3,1,0:T(8,128)(2,1)S(1)} %copy-done.2), kind=kOutput, calls=%fused_computation.72 | convolution fusion | flops 108527616 | bytes 4980736 | tf_op jit(solution)/shard_map/oc,pcxy->poxy/dot_general | solution.py:29
  128.2 2.5 %fusion.63 = f32[2,24,256,69]{2,3,1,0:T(8,128)} fusion(bf16[2,64,26,258]{3,1,2,0:T(8,128)(2,1)S(1)} %select_maximum_fusion, bf16[3,3,69,64]{2,3,1,0:T(8,128)(2,1)S(1)} %copy-done.2), kind=kOutput, calls=%fused_computation.74 | convolution fusion | flops 108527616 | bytes 4980736 | tf_op jit(solution)/shard_map/oc,pcxy->poxy/dot_general | solution.py:29
  130.8 2.5 %fusion.65 = f32[2,24,256,69]{2,3,1,0:T(8,128)} fusion(bf16[2,64,26,258]{3,1,2,0:T(8,128)(2,1)S(1)} %select_maximum_fusion, bf16[3,3,69,64]{2,3,1,0:T(8,128)(2,1)S(1)} %copy-done.2), kind=kOutput, calls=%fused_computation.76 | convolution fusion | flops 108527616 | bytes 4980736 | tf_op jit(solution)/shard_map/oc,pcxy->poxy/dot_general | solution.py:29
  133.3 2.4 %fusion.67 = f32[2,24,256,69]{2,3,1,0:T(8,128)} fusion(bf16[2,64,26,258]{3,1,2,0:T(8,128)(2,1)S(1)} %select_maximum_fusion, bf16[3,3,69,64]{2,3,1,0:T(8,128)(2,1)S(1)} %copy-done.2), kind=kOutput, calls=%fused_computation.78 | convolution fusion | flops 108527616 | bytes 4980736 | tf_op jit(solution)/shard_map/oc,pcxy->poxy/dot_general | solution.py:29
  135.7 2.4 %fusion.47 = f32[2,24,256,69]{2,3,1,0:T(8,128)} fusion(bf16[2,64,24,256]{3,1,2,0:T(8,128)(2,1)S(1)} %fusion.16, bf16[2,64,1,256]{3,1,2,0:T(8,128)(2,1)S(1)} %collective-permute-done.4, bf16[3,3,69,64]{2,3,1,0:T(8,128)(2,1)S(1)} %copy-done.2), kind=kOutput, calls=%fused_computation.60 | convolution fusion | flops 111804416 | bytes 5046272 | tf_op jit(solution)/shard_map/oc,pcxy->poxy/dot_general | solution.py:29
  138.1 2.4 %fusion.51 = f32[2,24,256,69]{2,3,1,0:T(8,128)} fusion(bf16[2,64,1,256]{3,1,2,0:T(8,128)(2,1)S(1)} %collective-permute-done.5, bf16[2,64,24,256]{3,1,2,0:T(8,128)(2,1)S(1)} %fusion.16, bf16[3,3,69,64]{2,3,1,0:T(8,128)(2,1)S(1)} %copy-done.2), kind=kOutput, calls=%fused_computation.64 | convolution fusion | flops 111804416 | bytes 5046272 | tf_op jit(solution)/shard_map/oc,pcxy->poxy/dot_general | solution.py:29
  140.5 10.1 %fusion.3 = bf16[2,69,24,256]{3,1,2,0:T(8,128)(2,1)S(1)} fusion(f32[2,24,256,69]{2,3,1,0:T(8,128)} %fusion.51, f32[2,24,256,69]{2,3,1,0:T(8,128)} %fusion.59, f32[2,24,256,69]{2,3,1,0:T(8,128)} %fusion.61, f32[2,24,256,69]{2,3,1,0:T(8,128)S(1)} %fusion.91, f32[2,24,256,69]{2,3,1,0:T(8,128)} %fusion.63, f32[2,24,256,69]{2,3,1,0:T(8,128)} %fusion.65, ...), kind=kOutput, calls=%fused_computation.11 | convolution fusion | flops 122941440 | bytes 34055168 | tf_op jit(solution)/shard_map/oc,pcxy->poxy/dot_general | solution.py:29
  (58 shorter events, 30.0 us)
Async XLA Ops:
  7.2 2.2 %copy-start = (bf16[2,69,24,256]{3,2,1,0:T(8,128)(2,1)S(1)}, bf16[2,69,24,256]{3,2,1,0:T(8,128)(2,1)}, u32[]{:S(2)}) copy-start(bf16[2,69,24,256]{3,2,1,0:T(8,128)(2,1)} %param.9) | copy-start | bytes 5087236
  7.2 2.1 %copy-start.5 = (s32[24,256]{1,0:T(8,128)S(1)}, s32[24,256]{1,0:T(8,128)}, u32[]{:S(2)}) copy-start(s32[24,256]{1,0:T(8,128)} %param.12) | copy-start | bytes 73732
  7.2 2.1 %copy-start.4 = (f32[24,256]{1,0:T(8,128)S(1)}, f32[24,256]{1,0:T(8,128)}, u32[]{:S(2)}) copy-start(f32[24,256]{1,0:T(8,128)} %param.11) | copy-start | bytes 73732
  7.2 54.4 %all-gather.2.cloned.1.call-start = ((), (), s32[]{:S(2)}) async-start(), calls=%async_computation | async-start | bytes 8478720 | tf_op jit(solution)/shard_map/all_gather | solution.py:55
  7.9 15.7 %copy-start.7 = (u32[32]{0:T(128)S(1)}, u32[32]{0:T(128)}, u32[]{:S(2)}) copy-start(u32[32]{0:T(128)} %constant.60) | copy-start | bytes 388
  7.9 28.4 %copy-start.6 = (s32[2]{0:T(128)S(1)}, s32[2]{0:T(128)}, u32[]{:S(2)}) copy-start(s32[2]{0:T(128)} %param.13) | copy-start | bytes 28
  65.2 4.4 %copy-start.3 = (bf16[3,3,64,69]{3,2,1,0:T(8,128)(2,1)S(1)}, bf16[3,3,64,69]{3,2,1,0:T(8,128)(2,1)}, u32[]{:S(2)}) copy-start(bf16[3,3,64,69]{3,2,1,0:T(8,128)(2,1)} %param.15) | copy-start | bytes 238468
  65.7 6.7 %collective-permute-start = (bf16[2,69,1,256]{3,1,2,0:T(8,128)(2,1)S(1)}, bf16[2,69,1,256]{3,1,2,0:T(8,128)(2,1)S(1)}, u32[]{:S(2)}, u32[]{:S(2)}) collective-permute-start(bf16[2,69,1,256]{3,1,2,0:T(8,128)(2,1)S(1)} %get-tuple-element.14), channel_id=1, source_target_pairs={{0,4},{4,8},{8,12},{12,0},{1,5},{5,9},{9,13},{13,1},{2,6},{6,10},{... | collective-permute-start | bytes 211976 | tf_op jit(solution)/shard_map/ppermute | solution.py:13
  67.2 5.7 %collective-permute-start.1 = (bf16[2,69,1,256]{3,1,2,0:T(8,128)(2,1)S(1)}, bf16[2,69,1,256]{3,1,2,0:T(8,128)(2,1)S(1)}, u32[]{:S(2)}, u32[]{:S(2)}) collective-permute-start(bf16[2,69,1,256]{3,1,2,0:T(8,128)(2,1)S(1)} %get-tuple-element.15), channel_id=1, source_target_pairs={{4,0},{8,4},{12,8},{0,12},{5,1},{9,5},{13,9},{1,13},{6,2},{10,6},{... | collective-permute-start | bytes 211976 | tf_op jit(solution)/shard_map/ppermute | solution.py:16
  84.4 9.9 %copy-start.1 = (bf16[3,3,64,64]{3,2,1,0:T(8,128)(2,1)S(1)}, bf16[3,3,64,64]{3,2,1,0:T(8,128)(2,1)}, u32[]{:S(2)}) copy-start(bf16[3,3,64,64]{3,2,1,0:T(8,128)(2,1)} %param.16) | copy-start | bytes 221188
  90.4 6.3 %collective-permute-start.2 = (bf16[2,64,1,256]{3,1,2,0:T(8,128)(2,1)S(1)}, bf16[2,64,1,256]{3,1,2,0:T(8,128)(2,1)S(1)}, u32[]{:S(2)}, u32[]{:S(2)}) collective-permute-start(bf16[2,64,1,256]{3,1,2,0:T(8,128)(2,1)S(1)} %get-tuple-element.18), channel_id=1, source_target_pairs={{0,4},{4,8},{8,12},{12,0},{1,5},{5,9},{9,13},{13,1},{2,6},{6,10},{... | collective-permute-start | bytes 196616 | tf_op jit(solution)/shard_map/ppermute | solution.py:13
  91.6 5.2 %collective-permute-start.3 = (bf16[2,64,1,256]{3,1,2,0:T(8,128)(2,1)S(1)}, bf16[2,64,1,256]{3,1,2,0:T(8,128)(2,1)S(1)}, u32[]{:S(2)}, u32[]{:S(2)}) collective-permute-start(bf16[2,64,1,256]{3,1,2,0:T(8,128)(2,1)S(1)} %get-tuple-element.19), channel_id=1, source_target_pairs={{4,0},{8,4},{12,8},{0,12},{5,1},{9,5},{13,9},{1,13},{6,2},{10,6},{... | collective-permute-start | bytes 196616 | tf_op jit(solution)/shard_map/ppermute | solution.py:16
  109.3 9.9 %copy-start.2 = (bf16[3,3,69,64]{2,3,1,0:T(8,128)(2,1)S(1)}, bf16[3,3,69,64]{2,3,1,0:T(8,128)(2,1)}, u32[]{:S(2)}) copy-start(bf16[3,3,69,64]{2,3,1,0:T(8,128)(2,1)} %param.17) | copy-start | bytes 238468
  115.3 6.2 %collective-permute-start.4 = (bf16[2,64,1,256]{3,1,2,0:T(8,128)(2,1)S(1)}, bf16[2,64,1,256]{3,1,2,0:T(8,128)(2,1)S(1)}, u32[]{:S(2)}, u32[]{:S(2)}) collective-permute-start(bf16[2,64,1,256]{3,1,2,0:T(8,128)(2,1)S(1)} %get-tuple-element.16), channel_id=1, source_target_pairs={{0,4},{4,8},{8,12},{12,0},{1,5},{5,9},{9,13},{13,1},{2,6},{6,10},{... | collective-permute-start | bytes 196616 | tf_op jit(solution)/shard_map/ppermute | solution.py:13
  115.9 5.6 %collective-permute-start.5 = (bf16[2,64,1,256]{3,1,2,0:T(8,128)(2,1)S(1)}, bf16[2,64,1,256]{3,1,2,0:T(8,128)(2,1)S(1)}, u32[]{:S(2)}, u32[]{:S(2)}) collective-permute-start(bf16[2,64,1,256]{3,1,2,0:T(8,128)(2,1)S(1)} %get-tuple-element.17), channel_id=1, source_target_pairs={{4,0},{8,4},{12,8},{0,12},{5,1},{9,5},{13,9},{1,13},{6,2},{10,6},{... | collective-permute-start | bytes 196616 | tf_op jit(solution)/shard_map/ppermute | solution.py:16
Sparse Core Ops, SparseCore 0:
  9.6 51.9 all-gather.1
where the time goes:
time: 159 us
  matrix products  63.2 us (40%)
  waiting for transfers between devices  30.2 us (19%)
  blocking collectives  19.6 us (12%)
  between operations  16.9 us (11%)
  starting transfers between devices  11.7 us (7%)
  other arithmetic  9.41 us (6%)
  local copies, waits for them, and re-layouts  7.92 us (5%)
    dot_general x27, matrix products, conv_local(): jnp.einsum('oc,pcxy->poxy', weight[row_tap, col_tap], window, preferred_e...  63.2 us
    all_gather x1, waiting for transfers between devices, continue_slots(): slab_piece = lax.all_gather(slabs, 'dom', axis=0, tiled=True)  25.2 us
    psum x1, blocking collectives, on_device(): band_sums = lax.psum(local_sums, 'lon')  13.4 us
    ppermute x3, starting transfers between devices, extended_2(): lax.ppermute(lax.slice_in_dim(block, 0, width, axis=dim), axis, backward)  8.36 us
    unnamed x1, blocking collectives  6.14 us
    concatenate x3, other arithmetic, extended_2(): block = jnp.concatenate([low, block, high], axis=dim)  5.59 us
    ppermute x3, waiting for transfers between devices, extended_2(): lax.ppermute(lax.slice_in_dim(block, block.shape[dim] - width, None, axis...  3.61 us
    gather x1, local copies, waits for them, and re-layouts, continue_slots(): jnp.take(slab_piece, jnp.clip(slot_ancestors, 0, piece_rows - 1), axis=0)  3.58 us
  transfers between devices with their start and end apart: 7, of which 6 were waited for; matrix products, arithmetic and copies ran while one was open for 6% of the time, Pallas kernels for 0%

commit v1 on v0

--- a/solution.py
+++ b/solution.py
@@ -52,7 +52,16 @@
 
 
 def continue_slots(slabs, slot_ancestors):
-    slab_piece = lax.all_gather(slabs, "dom", axis=0, tiled=True)
+    ways = lax.axis_size("dom")
+    up = [(d, (d + 1) % ways) for d in range(ways)]
+    down = [(d, (d - 1) % ways) for d in range(ways)]
+    earlier, later = ([slabs], [slabs])
+    for _ in range(ways // 2):
+        earlier.append(lax.ppermute(earlier[-1], "dom", up))
+    for _ in range((ways - 1) // 2):
+        later.append(lax.ppermute(later[-1], "dom", down))
+    line = jnp.concatenate([*earlier[::-1], *later[1:]], axis=0)
+    slab_piece = jnp.roll(line, (lax.axis_index("dom") - ways // 2) * slabs.shape[0], axis=0)
     piece_rows = slab_piece.shape[0]
     inside = (slot_ancestors >= 0) & (slot_ancestors < piece_rows)
     chosen = jnp.take(slab_piece, jnp.clip(slot_ancestors, 0, piece_rows - 1), axis=0)

time: 159 us -> 187 us (1.18)
  local copies, waits for them, and re-layouts: 7.92 us -> 33.3 us
  blocking collectives: 19.6 us -> 36.7 us
  between operations: 16.9 us -> 3.53 us
  waiting for transfers between devices: 30.2 us -> 25 us
  starting transfers between devices: 11.7 us -> 14.1 us
    all_gather x1 -> x0, waiting for transfers between devices: 25.2 us -> none  [continue_slots(): slab_piece = lax.all_gather(slabs, 'dom', axis=0, tiled=True)]
    ppermute x0 -> x3, waiting for transfers between devices: none -> 21.7 us  [the longest x2 21.7 us: continue_slots(): earlier.append(lax.ppermute(earlier[-1], 'dom', up))]
    unnamed x1, blocking collectives: 6.14 us -> 23.9 us
    unnamed x20 -> x23, local copies, waits for them, and re-layouts: 2.38 us -> 18.9 us
    dynamic_slice x0 -> x1, local copies, waits for them, and re-layouts: none -> 6.07 us  [continue_slots(): jnp.roll(line, (lax.axis_index('dom') - ways // 2) * slabs.shape[0], axis=0)]
    concatenate x0 -> x1, local copies, waits for them, and re-layouts: none -> 2.84 us  [continue_slots(): jnp.roll(line, (lax.axis_index('dom') - ways // 2) * slabs.shape[0], axis=0)]
    ppermute x0 -> x3, starting transfers between devices: none -> 2.25 us  [the longest x1 1.74 us: continue_slots(): later.append(lax.ppermute(later[-1], 'dom', down))]
  transfers between devices with their start and end apart: 7 -> 9, of which waited for: 6 -> 4; matrix products, arithmetic and copies ran while one was open for 6% -> 9% of each run, Pallas kernels for 0% -> 0%
where the time goes in v1:
time: 187 us; the launch traced here: 186 us
  matrix products  63.2 us (34%)
  blocking collectives  36.7 us (20%)
  local copies, waits for them, and re-layouts  33.3 us (18%)
  waiting for transfers between devices  25 us (13%)
  starting transfers between devices  14.1 us (8%)
  other arithmetic  10.2 us (5%)
  between operations  3.53 us (2%)
    dot_general x27, matrix products, conv_local(): jnp.einsum('oc,pcxy->poxy', weight[row_tap, col_tap], window, preferred_e...  63.2 us
    unnamed x1, blocking collectives  23.9 us
    ppermute x2, waiting for transfers between devices, continue_slots(): earlier.append(lax.ppermute(earlier[-1], 'dom', up))  21.7 us
    unnamed x23, local copies, waits for them, and re-layouts  18.9 us
    psum x1, blocking collectives, on_device(): band_sums = lax.psum(local_sums, 'lon')  12.8 us
    ppermute x3, starting transfers between devices, extended_2(): lax.ppermute(lax.slice_in_dim(block, 0, width, axis=dim), axis, backward)  8.15 us
    dynamic_slice x1, local copies, waits for them, and re-layouts, continue_slots(): jnp.roll(line, (lax.axis_index('dom') - ways // 2) * slabs.shape[0], axis=0)  6.07 us
    concatenate x3, other arithmetic, extended_2(): block = jnp.concatenate([low, block, high], axis=dim)  5.59 us
  transfers between devices with their start and end apart: 9, of which 4 were waited for; matrix products, arithmetic and copies ran while one was open for 9% of the time, Pallas kernels for 0%

profile of v1, /device:TPU:0, one launch (start us, length us, event | category | flops | bytes accessed | tf_op | source)
XLA Modules:
  0.0 186.0 jit_solution(8505134122628778350)
XLA Ops:
  1.1 21.7 %collective-permute-done = bf16[2,69,24,256]{3,2,1,0:T(8,128)(2,1)} collective-permute-done((bf16[2,69,24,256]{3,2,1,0:T(8,128)(2,1)}, bf16[2,69,24,256]{3,2,1,0:T(8,128)(2,1)}, u32[]{:S(2)}, u32[]{:S(2)}) %collective-permute-start) | collective-permute-done | bytes 1695776 | tf_op jit(solution)/shard_map/ppermute | solution.py:60
  27.6 12.8 %psum.7 = f32[2]{0:T(128)S(1)} all-reduce(f32[2]{0:T(128)S(1)} %fusion.5), channel_id=1, replica_groups=mesh['ens'=2,'lon'=4,'dom'=4] {'lon'}, use_global_device_ids=true, to_apply=%region_1.0 | all-reduce | flops 2 | bytes 16 | tf_op jit(solution)/shard_map/psum | solution.py:75
  41.8 23.9 %all-reduce.3 = f32[8]{0:T(128)S(1)} all-reduce(f32[8]{0:T(128)S(1)} %dynamic-update-slice), channel_id=1, replica_groups=mesh['ens'=2,'lon'=4,'dom'=4] {'dom'}, use_global_device_ids=true, to_apply=%add.3 | all-reduce | flops 8 | bytes 64
  70.9 2.7 %constant_dynamic-update-slice_fusion.7 = bf16[16,69,24,256]{3,2,1,0:T(8,128)(2,1)} fusion(bf16[2,69,24,256]{3,2,1,0:T(8,128)(2,1)} %collective-permute-done.1), kind=kLoop, calls=%fused_computation.106 | loop fusion | bytes 3391488
  73.6 2.7 %constant_dynamic-update-slice_fusion.6 = bf16[16,69,24,256]{3,2,1,0:T(8,128)(2,1)} fusion(bf16[16,69,24,256]{3,2,1,0:T(8,128)(2,1)} %constant_dynamic-update-slice_fusion.7, bf16[2,69,24,256]{3,2,1,0:T(8,128)(2,1)} %collective-permute-done), kind=kLoop, calls=%fused_computation.105 | loop fusion | bytes 3391488
  77.7 2.8 %constant_dynamic-update-slice_fusion.4 = bf16[16,69,24,256]{3,2,1,0:T(8,128)(2,1)} fusion(bf16[16,69,24,256]{3,2,1,0:T(8,128)(2,1)} %constant_dynamic-update-slice_fusion.5, bf16[2,69,24,256]{3,2,1,0:T(8,128)(2,1)} %collective-permute-done.2), kind=kLoop, calls=%fused_computation.103 | loop fusion | bytes 3391488
  80.5 2.8 %constant_dynamic-update-slice_fusion.3 = bf16[16,69,24,256]{3,2,1,0:T(8,128)(2,1)} fusion(bf16[16,69,24,256]{3,2,1,0:T(8,128)(2,1)} %constant_dynamic-update-slice_fusion.4, bf16[2,69,24,256]{3,2,1,0:T(8,128)(2,1)} %collective-permute-done.1), kind=kLoop, calls=%fused_computation.102 | loop fusion | bytes 3391488
  83.3 2.8 %constant_dynamic-update-slice_fusion.2 = bf16[16,69,24,256]{3,2,1,0:T(8,128)(2,1)} fusion(bf16[16,69,24,256]{3,2,1,0:T(8,128)(2,1)} %constant_dynamic-update-slice_fusion.3, bf16[2,69,24,256]{3,2,1,0:T(8,128)(2,1)} %collective-permute-done), kind=kLoop, calls=%fused_computation.101 | loop fusion | bytes 3391488
  87.4 2.8 %constant_dynamic-update-slice_fusion = bf16[16,69,24,256]{3,2,1,0:T(8,128)(2,1)} fusion(bf16[16,69,24,256]{3,2,1,0:T(8,128)(2,1)} %constant_dynamic-update-slice_fusion.1, bf16[2,69,24,256]{3,2,1,0:T(8,128)(2,1)} %collective-permute-done.2), kind=kLoop, calls=%fused_computation.99 | loop fusion | bytes 3391488 | tf_op jit(solution)/shard_map/jit(_roll_dynamic)/concatenate | solution.py:64
  90.2 6.1 %constant_dynamic-slice_fusion = bf16[8,69,24,256]{3,2,1,0:T(8,128)(2,1)} fusion(bf16[16,69,24,256]{3,2,1,0:T(8,128)(2,1)} %constant_dynamic-update-slice_fusion, s32[]{:T(128)S(6)} %select_n.31), kind=kLoop, calls=%fused_computation.172 | loop fusion | bytes 13565956 | tf_op jit(solution)/shard_map/jit(_roll_dynamic)/dynamic_slice | solution.py:64
  96.3 3.6 %gather_fusion = bf16[2,69,24,256]{3,2,1,0:T(8,128)(2,1)S(1)} fusion(bf16[8,69,24,256]{3,2,1,0:T(8,128)(2,1)} %constant_dynamic-slice_fusion, s32[1024]{0:T(1024)S(1)} %pad_clamp_fusion), kind=kCustom, calls=%fused_computation | custom fusion | bytes 3391496 | tf_op jit(solution)/shard_map/jit(_take)/gather | solution.py:67
  101.8 2.5 %collective-permute-start.4 = (bf16[2,69,1,256]{3,1,2,0:T(8,128)(2,1)S(1)}, bf16[2,69,1,256]{3,1,2,0:T(8,128)(2,1)S(1)}, u32[]{:S(2)}, u32[]{:S(2)}) collective-permute-start(bf16[2,69,1,256]{3,1,2,0:T(8,128)(2,1)S(1)} %get-tuple-element.13), channel_id=1, source_target_pairs={{4,0},{8,4},{12,8},{0,12},{5,1},{9,5},{13,9},{1,13},{6,2},{10,6},{... | collective-permute-start | bytes 211976 | tf_op jit(solution)/shard_map/ppermute | solution.py:16
  104.2 2.6 %fusion.111 = f32[2,24,256,64]{2,3,1,0:T(8,128)} fusion(bf16[3,3,64,69]{3,2,1,0:T(8,128)(2,1)S(1)} %copy-done.3, bf16[2,69,24,256]{3,2,1,0:T(8,128)(2,1)S(1)} %gather_fusion, pred[2]{0:T(512)(128)(4,1)S(1)} %get-tuple-element.10, pred[2]{0:T(512)(128)(4,1)S(1)} %get-tuple-element.18), kind=kOutput, calls=%fused_computation.131 | convolution fusion | flops 110223360 | bytes 4858880 | tf_op jit(solution)/shard_map/oc,pcxy->poxy/dot_general | solution.py:29
  118.4 6.0 %fusion.15 = bf16[2,64,24,256]{3,1,2,0:T(8,128)(2,1)S(1)} fusion(f32[2,24,256,64]{2,3,1,0:T(8,128)} %fusion.28, f32[2,24,256,64]{2,3,1,0:T(8,128)S(1)} %fusion.34, f32[2,24,256,64]{2,3,1,0:T(8,128)S(1)} %fusion.36, f32[2,24,256,64]{2,3,1,0:T(8,128)} %fusion.111, f32[2,24,256,64]{2,3,1,0:T(8,128)S(1)} %fusion.38, f32[2,24,256,64]{2,3,1,0:T(8,128)S(1)} %fusion.40, ...), kind=kOutput, calls=%fused_computation.27 | convolution fusion | flops 118751232 | bytes 28524544 | tf_op jit(solution)/shard_map/oc,pcxy->poxy/dot_general | solution.py:29
  125.5 2.8 %collective-permute-start.6 = (bf16[2,64,1,256]{3,1,2,0:T(8,128)(2,1)S(1)}, bf16[2,64,1,256]{3,1,2,0:T(8,128)(2,1)S(1)}, u32[]{:S(2)}, u32[]{:S(2)}) collective-permute-start(bf16[2,64,1,256]{3,1,2,0:T(8,128)(2,1)S(1)} %get-tuple-element.17), channel_id=1, source_target_pairs={{4,0},{8,4},{12,8},{0,12},{5,1},{9,5},{13,9},{1,13},{6,2},{10,6},{... | collective-permute-start | bytes 196616 | tf_op jit(solution)/shard_map/ppermute | solution.py:16
  143.1 5.9 %fusion.16 = bf16[2,64,24,256]{3,1,2,0:T(8,128)(2,1)S(1)} fusion(f32[2,24,256,64]{2,3,1,0:T(8,128)} %fusion.73, f32[2,24,256,64]{2,3,1,0:T(8,128)S(1)} %fusion.75, f32[2,24,256,64]{2,3,1,0:T(8,128)S(1)} %fusion.77, f32[2,24,256,64]{2,3,1,0:T(8,128)S(1)} %fusion.101, f32[2,24,256,64]{2,3,1,0:T(8,128)S(1)} %fusion.79, f32[2,24,256,64]{2,3,1,0:T(8,128)} %fusion.81, ...), kind=kOutput, calls=%fused_computation.28 | convolution fusion | flops 110886912 | bytes 28327936 | tf_op jit(solution)/shard_map/oc,pcxy->poxy/dot_general | solution.py:29
  150.3 2.9 %collective-permute-start.8 = (bf16[2,64,1,256]{3,1,2,0:T(8,128)(2,1)S(1)}, bf16[2,64,1,256]{3,1,2,0:T(8,128)(2,1)S(1)}, u32[]{:S(2)}, u32[]{:S(2)}) collective-permute-start(bf16[2,64,1,256]{3,1,2,0:T(8,128)(2,1)S(1)} %get-tuple-element.15), channel_id=1, source_target_pairs={{4,0},{8,4},{12,8},{0,12},{5,1},{9,5},{13,9},{1,13},{6,2},{10,6},{... | collective-permute-start | bytes 196616 | tf_op jit(solution)/shard_map/ppermute | solution.py:16
  157.1 2.5 %fusion.59 = f32[2,24,256,69]{2,3,1,0:T(8,128)} fusion(bf16[2,64,26,258]{3,1,2,0:T(8,128)(2,1)S(1)} %select_maximum_fusion, bf16[3,3,69,64]{2,3,1,0:T(8,128)(2,1)S(1)} %copy-done.2), kind=kOutput, calls=%fused_computation.70 | convolution fusion | flops 108527616 | bytes 4980736 | tf_op jit(solution)/shard_map/oc,pcxy->poxy/dot_general | solution.py:29
  159.5 2.6 %fusion.61 = f32[2,24,256,69]{2,3,1,0:T(8,128)} fusion(bf16[2,64,26,258]{3,1,2,0:T(8,128)(2,1)S(1)} %select_maximum_fusion, bf16[3,3,69,64]{2,3,1,0:T(8,128)(2,1)S(1)} %copy-done.2), kind=kOutput, calls=%fused_computation.72 | convolution fusion | flops 108527616 | bytes 4980736 | tf_op jit(solution)/shard_map/oc,pcxy->poxy/dot_general | solution.py:29
  162.1 2.5 %fusion.63 = f32[2,24,256,69]{2,3,1,0:T(8,128)} fusion(bf16[2,64,26,258]{3,1,2,0:T(8,128)(2,1)S(1)} %select_maximum_fusion, bf16[3,3,69,64]{2,3,1,0:T(8,128)(2,1)S(1)} %copy-done.2), kind=kOutput, calls=%fused_computation.74 | convolution fusion | flops 108527616 | bytes 4980736 | tf_op jit(solution)/shard_map/oc,pcxy->poxy/dot_general | solution.py:29
  164.7 2.5 %fusion.65 = f32[2,24,256,69]{2,3,1,0:T(8,128)} fusion(bf16[2,64,26,258]{3,1,2,0:T(8,128)(2,1)S(1)} %select_maximum_fusion, bf16[3,3,69,64]{2,3,1,0:T(8,128)(2,1)S(1)} %copy-done.2), kind=kOutput, calls=%fused_computation.76 | convolution fusion | flops 108527616 | bytes 4980736 | tf_op jit(solution)/shard_map/oc,pcxy->poxy/dot_general | solution.py:29
  167.1 2.4 %fusion.67 = f32[2,24,256,69]{2,3,1,0:T(8,128)} fusion(bf16[2,64,26,258]{3,1,2,0:T(8,128)(2,1)S(1)} %select_maximum_fusion, bf16[3,3,69,64]{2,3,1,0:T(8,128)(2,1)S(1)} %copy-done.2), kind=kOutput, calls=%fused_computation.78 | convolution fusion | flops 108527616 | bytes 4980736 | tf_op jit(solution)/shard_map/oc,pcxy->poxy/dot_general | solution.py:29
  169.5 2.4 %fusion.47 = f32[2,24,256,69]{2,3,1,0:T(8,128)} fusion(bf16[2,64,24,256]{3,1,2,0:T(8,128)(2,1)S(1)} %fusion.16, bf16[2,64,1,256]{3,1,2,0:T(8,128)(2,1)S(1)} %collective-permute-done.7, bf16[3,3,69,64]{2,3,1,0:T(8,128)(2,1)S(1)} %copy-done.2), kind=kOutput, calls=%fused_computation.60 | convolution fusion | flops 111804416 | bytes 5046272 | tf_op jit(solution)/shard_map/oc,pcxy->poxy/dot_general | solution.py:29
  174.4 10.1 %fusion.3 = bf16[2,69,24,256]{3,1,2,0:T(8,128)(2,1)S(1)} fusion(f32[2,24,256,69]{2,3,1,0:T(8,128)} %fusion.51, f32[2,24,256,69]{2,3,1,0:T(8,128)} %fusion.59, f32[2,24,256,69]{2,3,1,0:T(8,128)} %fusion.61, f32[2,24,256,69]{2,3,1,0:T(8,128)S(1)} %fusion.91, f32[2,24,256,69]{2,3,1,0:T(8,128)} %fusion.63, f32[2,24,256,69]{2,3,1,0:T(8,128)} %fusion.65, ...), kind=kOutput, calls=%fused_computation.11 | convolution fusion | flops 122941440 | bytes 34055168 | tf_op jit(solution)/shard_map/oc,pcxy->poxy/dot_general | solution.py:29
  (66 shorter events, 50.1 us)
Async XLA Ops:
  0.6 26.1 %copy-start = (bf16[2,69,24,256]{3,2,1,0:T(8,128)(2,1)S(1)}, bf16[2,69,24,256]{3,2,1,0:T(8,128)(2,1)}, u32[]{:S(2)}) copy-start(bf16[2,69,24,256]{3,2,1,0:T(8,128)(2,1)} %param.9) | copy-start | bytes 5087236
  0.6 22.2 %collective-permute-start = (bf16[2,69,24,256]{3,2,1,0:T(8,128)(2,1)}, bf16[2,69,24,256]{3,2,1,0:T(8,128)(2,1)}, u32[]{:S(2)}, u32[]{:S(2)}) collective-permute-start(bf16[2,69,24,256]{3,2,1,0:T(8,128)(2,1)} %param.9), channel_id=1, source_target_pairs={{0,1},{1,2},{2,3},{3,0},{4,5},{5,6},{6,7},{7,4},{8,9},{9,10},{10,1... | collective-permute-start | bytes 5087240 | tf_op jit(solution)/shard_map/ppermute | solution.py:60
  22.8 48.0 %collective-permute-start.1 = (bf16[2,69,24,256]{3,2,1,0:T(8,128)(2,1)}, bf16[2,69,24,256]{3,2,1,0:T(8,128)(2,1)}, u32[]{:S(2)}, u32[]{:S(2)}) collective-permute-start(bf16[2,69,24,256]{3,2,1,0:T(8,128)(2,1)} %collective-permute-done), channel_id=1, source_target_pairs={{0,1},{1,2},{2,3},{3,0},{4,5},{5,6},{6,7},{7,4},{8,9},{9,10},{10,1... | collective-permute-start | bytes 5087240 | tf_op jit(solution)/shard_map/ppermute | solution.py:60
  22.8 54.9 %collective-permute-start.2 = (bf16[2,69,24,256]{3,2,1,0:T(8,128)(2,1)}, bf16[2,69,24,256]{3,2,1,0:T(8,128)(2,1)}, u32[]{:S(2)}, u32[]{:S(2)}) collective-permute-start(bf16[2,69,24,256]{3,2,1,0:T(8,128)(2,1)} %param.9), channel_id=1, source_target_pairs={{0,3},{1,0},{2,1},{3,2},{4,7},{5,4},{6,5},{7,6},{8,11},{9,8},{10,9... | collective-permute-start | bytes 5087240 | tf_op jit(solution)/shard_map/ppermute | solution.py:62
  25.3 15.0 %copy-start.5 = (u32[32]{0:T(128)S(1)}, u32[32]{0:T(128)}, u32[]{:S(2)}) copy-start(u32[32]{0:T(128)} %constant.81) | copy-start | bytes 388
  25.3 45.5 %copy-start.4 = (s32[2]{0:T(128)S(1)}, s32[2]{0:T(128)}, u32[]{:S(2)}) copy-start(s32[2]{0:T(128)} %param.13) | copy-start | bytes 28
  99.9 4.4 %copy-start.3 = (bf16[3,3,64,69]{3,2,1,0:T(8,128)(2,1)S(1)}, bf16[3,3,64,69]{3,2,1,0:T(8,128)(2,1)}, u32[]{:S(2)}) copy-start(bf16[3,3,64,69]{3,2,1,0:T(8,128)(2,1)} %param.15) | copy-start | bytes 238468
  100.4 6.5 %collective-permute-start.3 = (bf16[2,69,1,256]{3,1,2,0:T(8,128)(2,1)S(1)}, bf16[2,69,1,256]{3,1,2,0:T(8,128)(2,1)S(1)}, u32[]{:S(2)}, u32[]{:S(2)}) collective-permute-start(bf16[2,69,1,256]{3,1,2,0:T(8,128)(2,1)S(1)} %get-tuple-element.12), channel_id=1, source_target_pairs={{0,4},{4,8},{8,12},{12,0},{1,5},{5,9},{9,13},{13,1},{2,6},{6,10},{... | collective-permute-start | bytes 211976 | tf_op jit(solution)/shard_map/ppermute | solution.py:13
  101.8 5.1 %collective-permute-start.4 = (bf16[2,69,1,256]{3,1,2,0:T(8,128)(2,1)S(1)}, bf16[2,69,1,256]{3,1,2,0:T(8,128)(2,1)S(1)}, u32[]{:S(2)}, u32[]{:S(2)}) collective-permute-start(bf16[2,69,1,256]{3,1,2,0:T(8,128)(2,1)S(1)} %get-tuple-element.13), channel_id=1, source_target_pairs={{4,0},{8,4},{12,8},{0,12},{5,1},{9,5},{13,9},{1,13},{6,2},{10,6},{... | collective-permute-start | bytes 211976 | tf_op jit(solution)/shard_map/ppermute | solution.py:16
  118.4 9.9 %copy-start.1 = (bf16[3,3,64,64]{3,2,1,0:T(8,128)(2,1)S(1)}, bf16[3,3,64,64]{3,2,1,0:T(8,128)(2,1)}, u32[]{:S(2)}) copy-start(bf16[3,3,64,64]{3,2,1,0:T(8,128)(2,1)} %param.16) | copy-start | bytes 221188
  124.4 6.2 %collective-permute-start.5 = (bf16[2,64,1,256]{3,1,2,0:T(8,128)(2,1)S(1)}, bf16[2,64,1,256]{3,1,2,0:T(8,128)(2,1)S(1)}, u32[]{:S(2)}, u32[]{:S(2)}) collective-permute-start(bf16[2,64,1,256]{3,1,2,0:T(8,128)(2,1)S(1)} %get-tuple-element.16), channel_id=1, source_target_pairs={{0,4},{4,8},{8,12},{12,0},{1,5},{5,9},{9,13},{13,1},{2,6},{6,10},{... | collective-permute-start | bytes 196616 | tf_op jit(solution)/shard_map/ppermute | solution.py:13
  125.5 5.1 %collective-permute-start.6 = (bf16[2,64,1,256]{3,1,2,0:T(8,128)(2,1)S(1)}, bf16[2,64,1,256]{3,1,2,0:T(8,128)(2,1)S(1)}, u32[]{:S(2)}, u32[]{:S(2)}) collective-permute-start(bf16[2,64,1,256]{3,1,2,0:T(8,128)(2,1)S(1)} %get-tuple-element.17), channel_id=1, source_target_pairs={{4,0},{8,4},{12,8},{0,12},{5,1},{9,5},{13,9},{1,13},{6,2},{10,6},{... | collective-permute-start | bytes 196616 | tf_op jit(solution)/shard_map/ppermute | solution.py:16
  143.1 10.0 %copy-start.2 = (bf16[3,3,69,64]{2,3,1,0:T(8,128)(2,1)S(1)}, bf16[3,3,69,64]{2,3,1,0:T(8,128)(2,1)}, u32[]{:S(2)}) copy-start(bf16[3,3,69,64]{2,3,1,0:T(8,128)(2,1)} %param.17) | copy-start | bytes 238468
  149.0 6.2 %collective-permute-start.7 = (bf16[2,64,1,256]{3,1,2,0:T(8,128)(2,1)S(1)}, bf16[2,64,1,256]{3,1,2,0:T(8,128)(2,1)S(1)}, u32[]{:S(2)}, u32[]{:S(2)}) collective-permute-start(bf16[2,64,1,256]{3,1,2,0:T(8,128)(2,1)S(1)} %get-tuple-element.14), channel_id=1, source_target_pairs={{0,4},{4,8},{8,12},{12,0},{1,5},{5,9},{9,13},{13,1},{2,6},{6,10},{... | collective-permute-start | bytes 196616 | tf_op jit(solution)/shard_map/ppermute | solution.py:13
  150.3 5.0 %collective-permute-start.8 = (bf16[2,64,1,256]{3,1,2,0:T(8,128)(2,1)S(1)}, bf16[2,64,1,256]{3,1,2,0:T(8,128)(2,1)S(1)}, u32[]{:S(2)}, u32[]{:S(2)}) collective-permute-start(bf16[2,64,1,256]{3,1,2,0:T(8,128)(2,1)S(1)} %get-tuple-element.15), channel_id=1, source_target_pairs={{4,0},{8,4},{12,8},{0,12},{5,1},{9,5},{13,9},{1,13},{6,2},{10,6},{... | collective-permute-start | bytes 196616 | tf_op jit(solution)/shard_map/ppermute | solution.py:16
